TPU v7x, 32 devices: a whole 2x2x4 slice. The times are simulated.
32 devices in a mesh: gx: 4 (over y, x), gy: 8 (over z, core).
Axes of the slice: x: 2, y: 2, z: 4, core: 2. Of those that a mesh axis runs over, the one named last changes fastest.
Arguments:
- inputs: bfloat16 [512, 8192], P('gx', 'gy'), may hold values from -6 to 6
- out_grad: bfloat16 [512, 8192], P('gx', 'gy'), may hold values from -1.1953125 to 1.1953125
- pre_act: bfloat16 [512, 32768], P('gy', 'gx'), may hold values from -6 to 6
- w_in: bfloat16 [8192, 32768], P('gy', 'gx'), may hold values from -0.0625 to 0.0625
- w_out: bfloat16 [32768, 8192], P('gx', 'gy'), may hold values from -0.03125 to 0.03125
- counts: int32 [4], replicated, may hold values from 1 to 128, 320 in all
Outputs:
- in_grad: bfloat16 [512, 8192], P('gx', 'gy')
- w_in_grad: bfloat16 [8192, 32768], P('gy', 'gx')
- w_out_grad: bfloat16 [32768, 8192], P('gx', 'gy')
Inputs may be any that keep to these rules, and one draw needn't show every extreme that they name: In batch shard s (token slots s * 128 to (s + 1) * 128 - 1) the first counts[s] slots are live and the rest are padding; the counts add up to exactly 320, and at least one shard is full.
All inputs are finite; a program needn't handle non-finite values.
Results may differ from a plain program's by a relative error of at most 0.0051.
Values may be sent and summed in bfloat16 or wider, within the bound.
No kernel may reach another device: no remote copies, remote signals or barrier semaphores. Data moves between devices by JAX's collectives and lax.ppermute only.
A program may use at most 192 MiB of HBM per device.

v0:
```python
import math
import jax
import jax.numpy as jnp
from jax import lax
from jax.sharding import PartitionSpec as P

gelu_scale = math.sqrt(2.0 / math.pi)
cubic_coef = 0.044715


def gelu_value(pre):
    tangent = jnp.tanh(gelu_scale * (pre + cubic_coef * pre * pre * pre))
    return 0.5 * pre * (1.0 + tangent)


def gelu_slope(pre):
    tangent = jnp.tanh(gelu_scale * (pre + cubic_coef * pre * pre * pre))
    return 0.5 * (1.0 + tangent) + 0.5 * pre * (1.0 - tangent * tangent) * gelu_scale * (
        1.0 + 3.0 * cubic_coef * pre * pre
    )


def token_sum(left, right):
    return lax.dot_general(
        left, right, (((0,), (0,)), ((), ())), preferred_element_type=jnp.float32
    )


def contract_last(left, right):
    return lax.dot_general(
        left, right, (((1,), (1,)), ((), ())), preferred_element_type=jnp.float32
    )


def live_mask(counts, shard_rows, all_rows, shards):
    positions = jnp.arange(all_rows, dtype=jnp.int32)
    owner_shard = positions // shard_rows
    one_hot = owner_shard[:, None] == jnp.arange(shards, dtype=jnp.int32)[None, :]
    own_count = jnp.sum(jnp.where(one_hot, counts[None, :], 0), axis=1)
    return positions % shard_rows < own_count


def packed_index(counts, shard_rows, shards, live_rows):
    ends = jnp.cumsum(counts)
    starts = ends - counts
    packed = jnp.arange(live_rows, dtype=jnp.int32)
    which = jnp.sum((ends[None, :] <= packed[:, None]).astype(jnp.int32), axis=1)
    one_hot = which[:, None] == jnp.arange(shards, dtype=jnp.int32)[None, :]
    begin = jnp.sum(jnp.where(one_hot, starts[None, :], 0), axis=1)
    return which * shard_rows + packed - begin


def body(inputs, out_grad, pre_act, w_in, w_out, counts):
    shard_rows = inputs.shape[0]
    shards = lax.axis_size("gx")
    all_rows = shard_rows * shards
    live_rows = all_rows * 5 // 8
    row_index = packed_index(counts, shard_rows, shards, live_rows)
    gathered_x, gathered_dy = (
        lax.all_gather(inputs, "gx", axis=0, tiled=True),
        lax.all_gather(out_grad, "gx", axis=0, tiled=True),
    )
    is_live = live_mask(counts, shard_rows, all_rows, shards)
    masked_grad = jnp.where(is_live[:, None], gathered_dy, jnp.zeros_like(gathered_dy))
    whole_pre = lax.all_gather(pre_act, "gy", axis=0, tiled=True).astype(jnp.float32)
    activation = gelu_value(whole_pre).astype(jnp.bfloat16)
    sent_grad = jnp.take(masked_grad, row_index, axis=0)
    sent_pre = jnp.take(whole_pre, row_index, axis=0)
    hidden_total = lax.psum(contract_last(sent_grad, w_out), "gy")
    sent_hidden = (hidden_total * gelu_slope(sent_pre)).astype(jnp.bfloat16)
    hidden_grad = (
        jnp.zeros((all_rows, sent_hidden.shape[1]), jnp.bfloat16).at[row_index].set(sent_hidden)
    )
    w_out_grad = token_sum(activation, masked_grad)
    w_in_grad = token_sum(gathered_x, hidden_grad)
    in_part = lax.psum_scatter(
        contract_last(hidden_grad, w_in), "gx", scatter_dimension=0, tiled=True
    )
    return (
        in_part.astype(jnp.bfloat16),
        w_in_grad.astype(jnp.bfloat16),
        w_out_grad.astype(jnp.bfloat16),
    )


def solution(mesh):
    return jax.shard_map(
        body,
        mesh=mesh,
        in_specs=(P("gx", "gy"), P("gx", "gy"), P("gy", "gx"), P("gy", "gx"), P("gx", "gy"), P()),
        out_specs=(P("gx", "gy"), P("gy", "gx"), P("gx", "gy")),
        check_vma=False,
    )
```

profile of v0, /device:TPU:0, one launch (start us, length us, event | category | flops | bytes accessed | tf_op | source)
XLA Modules:
  0.0 445.9 jit_solution(4498768962344689414)
XLA Ops:
  7.2 0.0 all-gather.4.cloned.1.call-start
  7.2 0.7 all-gather.4.cloned.1.call-update
  7.9 0.0 all-gather.6.cloned.1.call-start
  7.9 0.7 all-gather.6.cloned.1.call-update
  8.6 0.0 all-reduce.2.cloned.1.call-start
  8.7 0.8 reduce-window.8
  9.5 0.1 convert_reduce_fusion
  9.6 0.7 bitcast_subtract_fusion
  10.3 0.1 select_reduce_fusion.1
  10.4 0.7 select_reduce_fusion
  11.2 27.9 %all-gather.4.cloned.1.call-done = bf16[512,1024]{1,0:T(8,128)(2,1)} async-done(((bf16[128,1024]{1,0:T(8,128)(2,1)}), bf16[512,1024]{1,0:T(8,128)(2,1)}) %all-gather.4.cloned.1.call-update) | async-done | bytes 1048592 | tf_op jit(solution)/shard_map/all_gather | solution.py:61
  39.1 1.4 broadcast_select_fusion
  40.5 2.1 gather_fusion
  42.6 19.9 %fusion.20 = f32[320,8192]{1,0:T(8,128)} fusion(bf16[8192,1024]{1,0:T(8,128)(2,1)} %param.10, bf16[320,1024]{1,0:T(8,128)(2,1)S(1)} %gather_fusion, pred[320]{0:T(512)(128)(4,1)S(1)} %compare_and_fusion), kind=kOutput, calls=%fused_computation.28 | convolution fusion | flops 5369036800 | bytes 27918656 | tf_op jit(solution)/shard_map/dot_general | solution.py:30
  62.5 0.0 all-reduce.2.cloned.1.call-update
  62.5 0.0 all-gather.8.cloned.1.call-start
  62.6 0.5 all-gather.8.cloned.1.call-update
  63.1 0.3 reduce-scatter.2.cloned.1.call-start
  63.5 59.3 %all-gather.6.cloned.1.call-done = bf16[512,8192]{1,0:T(8,128)(2,1)} async-done(((bf16[64,8192]{1,0:T(8,128)(2,1)}), bf16[512,8192]{1,0:T(8,128)(2,1)}) %all-gather.6.cloned.1.call-update) | async-done | bytes 8388624 | tf_op jit(solution)/shard_map/all_gather | solution.py:65
  122.8 12.1 %convert_element_type.25 = f32[512,8192]{1,0:T(8,128)} convert(bf16[512,8192]{1,0:T(8,128)(2,1)} %all-gather.6.cloned.1.call-done) | non-fusion elementwise | flops 4194304 | bytes 25165824 | tf_op jit(solution)/shard_map/convert_element_type | solution.py:65
  134.9 19.9 %gather_fusion.1 = f32[320,8192]{1,0:T(8,128)} fusion(f32[512,8192]{1,0:T(8,128)} %convert_element_type.25, s32[1024]{0:T(1024)S(1)} %pad_clamp_fusion), kind=kCustom, calls=%fused_computation.1 | custom fusion | bytes 20972800 | tf_op jit(solution)/shard_map/jit(_take)/gather | solution.py:68
  154.8 184.5 %all-reduce.2.cloned.1.call-done = f32[320,8192]{1,0:T(8,128)} async-done(((f32[320,8192]{1,0:T(8,128)}), f32[320,8192]{1,0:T(8,128)}) %all-reduce.2.cloned.1.call-update) | async-done | bytes 10485776 | tf_op jit(solution)/shard_map/psum | solution.py:69
  339.3 12.5 %fusion.11 = bf16[320,8192]{1,0:T(8,128)(2,1)} fusion(f32[320,8192]{1,0:T(8,128)} %all-reduce.2.cloned.1.call-done, f32[320,8192]{1,0:T(8,128)} %gather_fusion.1, pred[320]{0:T(512)(128)(4,1)S(1)} %compare_and_fusion), kind=kLoop, calls=%fused_computation.19 | loop fusion | flops 52428800 | bytes 26214720 | tf_op jit(solution)/shard_map/convert_element_type | solution.py:70
  351.8 14.5 %scatter_custom_fusion = bf16[512,8192]{1,0:T(8,128)(2,1)} fusion(s32[320]{0:T(512)S(1)} %fusion.30, bf16[320,8192]{1,0:T(8,128)(2,1)} %fusion.11, bf16[]{:T(256)} %constant.45.clone.1), kind=kCustom, calls=%fused_computation.25 | custom fusion | bytes 8389120 | tf_op jit(solution)/shard_map/scatter | solution.py:72
  366.3 16.0 %fusion.36 = f32[512,1024]{1,0:T(8,128)} fusion(bf16[512,8192]{1,0:T(8,128)(2,1)} %scatter_custom_fusion, bf16[1024,8192]{1,0:T(8,128)(2,1)} %param.9), kind=kOutput, calls=%fused_computation.61 | convolution fusion | flops 8589934592 | bytes 27262976 | tf_op jit(solution)/shard_map/dot_general | solution.py:30
  382.3 0.0 reduce-scatter.2.cloned.1.call-update
  382.3 0.0 all-gather.8.cloned.1.call-done
  382.4 15.1 %convert_bitcast_fusion = bf16[1024,8192]{0,1:T(8,128)(2,1)} fusion(bf16[512,8192]{1,0:T(8,128)(2,1)} %scatter_custom_fusion, bf16[512,1024]{1,0:T(8,128)(2,1)} %all-gather.8.cloned.1.call-done), kind=kOutput, calls=%fused_computation.9 | convolution fusion | flops 8598323200 | bytes 26214400 | tf_op jit(solution)/shard_map/dot_general | solution.py:24
  397.4 21.3 %copy.11 = bf16[1024,8192]{1,0:T(8,128)(2,1)} copy(bf16[1024,8192]{0,1:T(8,128)(2,1)} %convert_bitcast_fusion) | data formatting | bytes 33554432
  418.7 18.7 %convolution_convert_fusion = bf16[8192,1024]{1,0:T(8,128)(2,1)} fusion(bf16[512,1024]{1,0:T(8,128)(2,1)S(1)} %broadcast_select_fusion, bf16[512,8192]{1,0:T(8,128)(2,1)} %all-gather.6.cloned.1.call-done), kind=kOutput, calls=%fused_computation.12 | convolution fusion | flops 8640266240 | bytes 26214400 | tf_op jit(solution)/shard_map/dot_general | solution.py:24
  437.4 0.0 reduce-scatter.2.cloned.1.call-done
  437.4 1.8 convert_element_type.27
  (6 shorter events, 0.1 us)
Async XLA Ops:
  7.2 31.9 %all-gather.4.cloned.1.call-start = ((), (), s32[]{:S(2)}) async-start(), calls=%async_computation.1 | async-start | bytes 1310720 | tf_op jit(solution)/shard_map/all_gather | solution.py:61
  7.9 114.9 %all-gather.6.cloned.1.call-start = ((), (), s32[]{:S(2)}) async-start(), calls=%async_computation.3 | async-start | bytes 9437184 | tf_op jit(solution)/shard_map/all_gather | solution.py:65
  8.6 330.6 %all-reduce.2.cloned.1.call-start = ((), (), s32[]{:S(2)}) async-start(), calls=%async_computation.2 | async-start | bytes 20971520 | tf_op jit(solution)/shard_map/psum | solution.py:69
  62.5 319.8 %all-gather.8.cloned.1.call-start = ((), (), s32[]{:S(2)}) async-start(), calls=%async_computation.5 | async-start | bytes 1310720 | tf_op jit(solution)/shard_map/all_gather | solution.py:60
  63.1 374.3 %reduce-scatter.2.cloned.1.call-start = ((), (), s32[]{:S(2)}) async-start(), calls=%async_computation.4 | async-start | bytes 2621440 | tf_op jit(solution)/shard_map/reduce_scatter | solution.py:76
Sparse Core Ops, SparseCore 0:
  9.8 29.2 all-gather.3
  40.7 82.0 all-gather.5
  125.7 213.5 all-reduce.1
  341.0 26.6 all-gather.7
  382.4 35.3 reduce-scatter.1
where the time goes:
time: 451 us; the launch traced here: 446 us
  waiting for transfers between devices  274 us (61%)
  matrix products  69.7 us (15%)
  local copies, waits for them, and re-layouts  57.8 us (13%)
  other arithmetic  30.2 us (7%)
  between operations  14.1 us (3%)
    psum x1, waiting for transfers between devices, body(): hidden_total = lax.psum(contract_last(sent_grad, w_out), 'gy')  185 us
    all_gather x1, waiting for transfers between devices, body(): lax.all_gather(pre_act, 'gy', axis=0, tiled=True).astype(jnp.float32)  59.3 us
    dot_general x2, matrix products, contract_last(): lax.dot_general(left, right, (((1,), (1,)), ((), ())), preferred_element_...  35.9 us
    dot_general x2, matrix products, token_sum(): lax.dot_general(left, right, (((0,), (0,)), ((), ())), preferred_element_...  33.7 us
    all_gather x1, waiting for transfers between devices, body(): lax.all_gather(out_grad, 'gx', axis=0, tiled=True)  27.9 us
    unnamed x1, local copies, waits for them, and re-layouts  21.3 us
    gather x1, local copies, waits for them, and re-layouts, body(): sent_pre = jnp.take(whole_pre, row_index, axis=0)  19.9 us
    scatter x1, local copies, waits for them, and re-layouts, body(): jnp.zeros((all_rows, sent_hidden.shape[1]), jnp.bfloat16).at[row_index]  14.5 us
  transfers between devices with their start and end apart: 5, of which 3 were waited for; matrix products, arithmetic and copies ran while one was open for 35% of the time, Pallas kernels for 0%

commit v1 on v0

--- a/solution.py
+++ b/solution.py
@@ -66,7 +66,9 @@
     activation = gelu_value(whole_pre).astype(jnp.bfloat16)
     sent_grad = jnp.take(masked_grad, row_index, axis=0)
     sent_pre = jnp.take(whole_pre, row_index, axis=0)
-    hidden_total = lax.psum(contract_last(sent_grad, w_out), "gy")
+    part = contract_last(sent_grad, w_out)
+    shards_2 = lax.all_gather(part, "gy")
+    hidden_total = jnp.sum(shards_2, axis=0)
     sent_hidden = (hidden_total * gelu_slope(sent_pre)).astype(jnp.bfloat16)
     hidden_grad = (
         jnp.zeros((all_rows, sent_hidden.shape[1]), jnp.bfloat16).at[row_index].set(sent_hidden)

time: 451 us -> 969 us (2.15)
  waiting for transfers between devices: 274 us -> 753 us
  other arithmetic: 30.2 us -> 64.9 us
    all_gather x0 -> x1, waiting for transfers between devices: none -> 663 us  [body(): shards_2 = lax.all_gather(part, 'gy')]
    psum x1 -> x0, waiting for transfers between devices: 185 us -> none  [body(): hidden_total = lax.psum(contract_last(sent_grad, w_out), 'gy')]
    reduce_sum x0 -> x1, other arithmetic: none -> 30.6 us  [body(): hidden_total = jnp.sum(shards_2, axis=0)]
  transfers between devices with their start and end apart: 5 -> 5, of which waited for: 3 -> 3; matrix products, arithmetic and copies ran while one was open for 35% -> 20% of each run, Pallas kernels for 0% -> 0%
where the time goes in v1:
time: 969 us; the launch traced here: 963 us
  waiting for transfers between devices  753 us (78%)
  matrix products  69.6 us (7%)
  other arithmetic  64.9 us (7%)
  local copies, waits for them, and re-layouts  61.5 us (6%)
  between operations  14.1 us (1%)
    all_gather x1, waiting for transfers between devices, body(): shards_2 = lax.all_gather(part, 'gy')  663 us
    all_gather x1, waiting for transfers between devices, body(): lax.all_gather(pre_act, 'gy', axis=0, tiled=True).astype(jnp.float32)  59.6 us
    dot_general x2, matrix products, contract_last(): lax.dot_general(left, right, (((1,), (1,)), ((), ())), preferred_element_...  36 us
    dot_general x2, matrix products, token_sum(): lax.dot_general(left, right, (((0,), (0,)), ((), ())), preferred_element_...  33.6 us
    reduce_sum x1, other arithmetic, body(): hidden_total = jnp.sum(shards_2, axis=0)  30.6 us
    all_gather x1, waiting for transfers between devices, body(): lax.all_gather(out_grad, 'gx', axis=0, tiled=True)  27.9 us
    gather x1, local copies, waits for them, and re-layouts, body(): sent_pre = jnp.take(whole_pre, row_index, axis=0)  24 us
    unnamed x1, local copies, waits for them, and re-layouts  21.2 us
  transfers between devices with their start and end apart: 5, of which 3 were waited for; matrix products, arithmetic and copies ran while one was open for 20% of the time, Pallas kernels for 0%

profile of v1, /device:TPU:0, one launch (start us, length us, event | category | flops | bytes accessed | tf_op | source)
XLA Modules:
  0.0 963.1 jit_solution(4625633025669767278)
XLA Ops:
  7.2 0.0 all-gather.6.cloned.1.call-start
  7.2 0.7 all-gather.6.cloned.1.call-update
  7.9 0.0 all-gather.8.cloned.1.call-start
  7.9 0.7 all-gather.8.cloned.1.call-update
  8.6 0.0 all-gather.12.cloned.1.call-start
  8.7 0.8 reduce-window.8
  9.5 0.1 convert_reduce_fusion
  9.6 0.7 bitcast_subtract_fusion
  10.3 0.1 select_reduce_fusion.1
  10.4 0.7 select_reduce_fusion
  11.2 27.9 %all-gather.6.cloned.1.call-done = bf16[512,1024]{1,0:T(8,128)(2,1)} async-done(((bf16[128,1024]{1,0:T(8,128)(2,1)}), bf16[512,1024]{1,0:T(8,128)(2,1)}) %all-gather.6.cloned.1.call-update) | async-done | bytes 1048592 | tf_op jit(solution)/shard_map/all_gather | solution.py:61
  39.1 1.4 broadcast_select_fusion
  40.5 2.1 gather_fusion
  42.6 19.9 %fusion.20 = f32[320,8192]{1,0:T(8,128)} fusion(bf16[8192,1024]{1,0:T(8,128)(2,1)} %param.10, bf16[320,1024]{1,0:T(8,128)(2,1)S(1)} %gather_fusion, pred[320]{0:T(512)(128)(4,1)S(1)} %compare_and_fusion), kind=kOutput, calls=%fused_computation.28 | convolution fusion | flops 5369036800 | bytes 27918656 | tf_op jit(solution)/shard_map/dot_general | solution.py:30
  62.5 0.0 all-gather.12.cloned.1.call-update
  62.5 0.0 all-gather.10.cloned.1.call-start
  62.6 0.5 all-gather.10.cloned.1.call-update
  63.1 0.0 reduce-scatter.2.cloned.1.call-start
  63.2 59.6 %all-gather.8.cloned.1.call-done = bf16[512,8192]{1,0:T(8,128)(2,1)} async-done(((bf16[64,8192]{1,0:T(8,128)(2,1)}), bf16[512,8192]{1,0:T(8,128)(2,1)}) %all-gather.8.cloned.1.call-update) | async-done | bytes 8388624 | tf_op jit(solution)/shard_map/all_gather | solution.py:65
  122.8 16.1 %convert_element_type.25 = f32[512,8192]{1,0:T(8,128)} convert(bf16[512,8192]{1,0:T(8,128)(2,1)} %all-gather.8.cloned.1.call-done) | non-fusion elementwise | flops 4194304 | bytes 25165824 | tf_op jit(solution)/shard_map/convert_element_type | solution.py:65
  138.9 24.0 %gather_fusion.1 = f32[320,8192]{1,0:T(8,128)} fusion(f32[512,8192]{1,0:T(8,128)} %convert_element_type.25, s32[1024]{0:T(1024)S(1)} %pad_clamp_fusion), kind=kCustom, calls=%fused_computation.1 | custom fusion | bytes 20972800 | tf_op jit(solution)/shard_map/jit(_take)/gather | solution.py:68
  162.9 663.4 %all-gather.12.cloned.1.call-done = f32[2560,8192]{1,0:T(8,128)} async-done(((f32[320,8192]{1,0:T(8,128)}), f32[2560,8192]{1,0:T(8,128)}) %all-gather.12.cloned.1.call-update) | async-done | bytes 83886096 | tf_op jit(solution)/shard_map/all_gather | solution.py:70
  826.3 30.6 %reduce_sum.42 = f32[320,8192]{1,0:T(8,128)} reduce(f32[8,320,8192]{2,1,0:T(8,128)} %bitcast.2, f32[]{:T(128)} %constant.78.clone.1), dimensions={0}, to_apply=%region_4.5 | reduce | flops 18350080 | bytes 94371840 | tf_op jit(solution)/shard_map/reduce_sum | solution.py:71
  856.9 12.5 %fusion.11 = bf16[320,8192]{1,0:T(8,128)(2,1)} fusion(f32[320,8192]{1,0:T(8,128)} %reduce_sum.42, f32[320,8192]{1,0:T(8,128)} %gather_fusion.1, pred[320]{0:T(512)(128)(4,1)S(1)} %compare_and_fusion), kind=kLoop, calls=%fused_computation.19 | loop fusion | flops 52428800 | bytes 26214720 | tf_op jit(solution)/shard_map/convert_element_type | solution.py:72
  869.4 14.2 %scatter_custom_fusion = bf16[512,8192]{1,0:T(8,128)(2,1)} fusion(s32[320]{0:T(512)S(1)} %fusion.30, bf16[320,8192]{1,0:T(8,128)(2,1)} %fusion.11, bf16[]{:T(256)} %constant.45.clone.1), kind=kCustom, calls=%fused_computation.25 | custom fusion | bytes 8389120 | tf_op jit(solution)/shard_map/scatter | solution.py:74
  883.6 16.0 %fusion.36 = f32[512,1024]{1,0:T(8,128)} fusion(bf16[512,8192]{1,0:T(8,128)(2,1)} %scatter_custom_fusion, bf16[1024,8192]{1,0:T(8,128)(2,1)} %param.9), kind=kOutput, calls=%fused_computation.61 | convolution fusion | flops 8589934592 | bytes 27262976 | tf_op jit(solution)/shard_map/dot_general | solution.py:30
  899.6 0.0 reduce-scatter.2.cloned.1.call-update
  899.7 18.5 %convolution_convert_fusion = bf16[8192,1024]{1,0:T(8,128)(2,1)} fusion(bf16[512,1024]{1,0:T(8,128)(2,1)S(1)} %broadcast_select_fusion, bf16[512,8192]{1,0:T(8,128)(2,1)} %all-gather.8.cloned.1.call-done), kind=kOutput, calls=%fused_computation.12 | convolution fusion | flops 8640266240 | bytes 26214400 | tf_op jit(solution)/shard_map/dot_general | solution.py:24
  918.2 0.0 all-gather.10.cloned.1.call-done
  918.2 15.1 %convert_bitcast_fusion = bf16[1024,8192]{0,1:T(8,128)(2,1)} fusion(bf16[512,8192]{1,0:T(8,128)(2,1)} %scatter_custom_fusion, bf16[512,1024]{1,0:T(8,128)(2,1)} %all-gather.10.cloned.1.call-done), kind=kOutput, calls=%fused_computation.9 | convolution fusion | flops 8598323200 | bytes 26214400 | tf_op jit(solution)/shard_map/dot_general | solution.py:24
  933.3 21.2 %copy.11 = bf16[1024,8192]{1,0:T(8,128)(2,1)} copy(bf16[1024,8192]{0,1:T(8,128)(2,1)} %convert_bitcast_fusion) | data formatting | bytes 33554432
  954.5 1.8 convert_element_type.27
  (7 shorter events, 0.1 us)
Async XLA Ops:
  7.2 31.9 %all-gather.6.cloned.1.call-start = ((), (), s32[]{:S(2)}) async-start(), calls=%async_computation.1 | async-start | bytes 1310720 | tf_op jit(solution)/shard_map/all_gather | solution.py:61
  7.9 114.9 %all-gather.8.cloned.1.call-start = ((), (), s32[]{:S(2)}) async-start(), calls=%async_computation.2 | async-start | bytes 9437184 | tf_op jit(solution)/shard_map/all_gather | solution.py:65
  8.6 817.6 %all-gather.12.cloned.1.call-start = ((), (), s32[]{:S(2)}) async-start(), calls=%async_computation.5 | async-start | bytes 94371840 | tf_op jit(solution)/shard_map/all_gather | solution.py:70
  62.5 855.6 %all-gather.10.cloned.1.call-start = ((), (), s32[]{:S(2)}) async-start(), calls=%async_computation.4 | async-start | bytes 1310720 | tf_op jit(solution)/shard_map/all_gather | solution.py:60
  63.1 891.4 %reduce-scatter.2.cloned.1.call-start = ((), (), s32[]{:S(2)}) async-start(), calls=%async_computation.3 | async-start | bytes 2621440 | tf_op jit(solution)/shard_map/reduce_scatter | solution.py:78
Sparse Core Ops, SparseCore 0:
  9.8 29.2 all-gather.5
  40.7 82.0 all-gather.7
  125.0 701.2 all-gather.11
  828.0 24.6 all-gather.9
  899.8 33.3 reduce-scatter.1
